TPU v7x, 32 devices: a whole 2x2x4 slice. The times are simulated.
32 devices in a mesh: grp: 2 (over x), seq: 4 (over y, core), sub: 4 (over z).
Axes of the slice: x: 2, y: 2, z: 4, core: 2. Of those that a mesh axis runs over, the one named last changes fastest.
Arguments:
- query_rows: bfloat16 [8, 512, 2048], P(('grp', 'sub'), 'seq'), parts along dimension 0, may hold values from -9 to 9
- key_rows: bfloat16 [8, 512, 256], P(('grp', 'sub'), 'seq'), parts along dimension 0, may hold values from -4 to 4
- value_rows: bfloat16 [8, 512, 256], P(('grp', 'sub'), 'seq'), parts along dimension 0, may hold values from -6 to 6
- residual_in: bfloat16 [8, 512, 2048], P(('grp', 'sub'), 'seq'), parts along dimension 0, may hold values from -6 to 6
- out_proj: bfloat16 [2048, 2048], P('seq'), may hold values from -0.5 to 0.5
- norm_gain: bfloat16 [2048], replicated, may hold values from 0.099609375 to 1.8984375
- expert_ids: int32 [8, 512, 8], P(('grp', 'sub'), 'seq'), parts along dimension 0, may hold values from 0 to 15, all different within a row; in each aligned block of 128 rows (0 to 127, 128 to 255, ..., all dimensions but the last counted through in order) at most 80 rows name the same one
- gate_weights: bfloat16 [8, 512, 8], P(('grp', 'sub'), 'seq'), parts along dimension 0, may hold values from 0.049804688 to 1
- expert_gate: bfloat16 [16, 2048, 768], P(('seq', 'sub')), may hold values from -0.125 to 0.125
- expert_up: bfloat16 [16, 2048, 768], P(('seq', 'sub')), may hold values from -0.125 to 0.125
- expert_down: bfloat16 [16, 768, 2048], P(('seq', 'sub')), may hold values from -0.21875 to 0.21875
Outputs:
- layer_out: bfloat16 [8, 512, 2048], P(('grp', 'sub'), 'seq'), parts along dimension 0
There are 2 independent parts, one for each index of `grp`. A program takes and returns all parts, laid end to end along the dimension named above; an argument that names none is the same for every part. Nothing has to cross between parts.
Inputs may be any that keep to these rules, and one draw needn't show every extreme that they name: `expert_ids`: A row names 8 different experts. In each aligned block of 128 rows (the rows of one device) no expert is named by more than 80 rows, a bound that some block reaches.
All inputs are finite; a program needn't handle non-finite values.
Results may differ from a plain program's by a relative error of at most 0.013.
Values may be sent and summed in bfloat16 or wider, within the bound.
A program may use at most 128 MiB of HBM per device.

v0:
```python
import jax
import jax.numpy as jnp
from jax import lax
from jax.sharding import PartitionSpec as P

D = 2048
HD = 128
QH = 16
KVH = 2


def attend_head(queries, keys_one, values_one, block):
    length = queries.shape[0]
    scale = 1.0 / queries.shape[1] ** 0.5
    pieces = []
    for part_index in range(length // block):
        stop = (part_index + 1) * block
        rows_here = queries[part_index * block : stop]
        scores = (
            jnp.einsum("qd,kd->qk", rows_here, keys_one[:stop], preferred_element_type=jnp.float32)
            * scale
        )
        row_pos = part_index * block + jnp.arange(block, dtype=jnp.int32)
        col_pos = jnp.arange(stop, dtype=jnp.int32)
        scores = jnp.where(row_pos[:, None] >= col_pos[None, :], scores, -1e30)
        peak = jnp.max(scores, axis=1, keepdims=True)
        weights = jnp.exp(scores - peak)
        probs = (weights / jnp.sum(weights, axis=1, keepdims=True)).astype(jnp.bfloat16)
        pieces.append(
            jnp.dot(probs, values_one[:stop], preferred_element_type=jnp.float32).astype(
                jnp.bfloat16
            )
        )
    return jnp.concatenate(pieces, axis=0)


def rank_in_expert(flat_ids, experts):
    items = flat_ids.shape[0]
    width = 128
    n_parts = items // width
    onehot = (
        (flat_ids[:, None] == jnp.arange(experts, dtype=jnp.int32)[None, :])
        .astype(jnp.bfloat16)
        .reshape(n_parts, width, experts)
    )
    lower = (
        jnp.arange(width, dtype=jnp.int32)[:, None] > jnp.arange(width, dtype=jnp.int32)[None, :]
    ).astype(jnp.bfloat16)
    within = jnp.einsum("ij,bje->bie", lower, onehot, preferred_element_type=jnp.float32)
    part_counts = jnp.sum(onehot.astype(jnp.float32), axis=1)
    earlier = jnp.cumsum(part_counts, axis=0) - part_counts
    ranks = jnp.sum((within + earlier[:, None, :]) * onehot.astype(jnp.float32), axis=2)
    return ranks.reshape(items).astype(jnp.int32)


def per_device(
    query_rows,
    key_rows,
    value_rows,
    residual_in,
    out_proj,
    norm_gain,
    expert_ids,
    gate_weights,
    expert_gate,
    expert_up,
    expert_down,
):
    tokens = query_rows.shape[1]
    n_seq = lax.axis_size("seq")
    n_sub = lax.axis_size("sub")
    heads_here = QH // n_seq
    group = QH // KVH
    query_local = lax.all_to_all(query_rows, "seq", split_axis=2, concat_axis=1, tiled=True)
    key_full, value_full = (
        lax.all_gather(key_rows, "seq", axis=1, tiled=True),
        lax.all_gather(value_rows, "seq", axis=1, tiled=True),
    )
    first_head = lax.axis_index("seq") * heads_here
    key_list = []
    value_list = []
    for head in range(heads_here):
        kv_start = (first_head + head) // group * HD
        key_list.append(lax.dynamic_slice_in_dim(key_full[0], kv_start, HD, 1))
        value_list.append(lax.dynamic_slice_in_dim(value_full[0], kv_start, HD, 1))
    length = query_local.shape[1]
    block = min(length, max(512, length // 8))
    outputs = [
        attend_head(
            query_local[0, :, head * HD : (head + 1) * HD], key_list[head], value_list[head], block
        )
        for head in range(heads_here)
    ]
    head_block = jnp.concatenate(outputs, axis=1)[None]
    attended = lax.all_to_all(head_block, "seq", split_axis=1, concat_axis=2, tiled=True)[0]
    projected = jnp.dot(
        attended,
        lax.all_gather(out_proj, "seq", axis=0, tiled=True),
        preferred_element_type=jnp.float32,
    )
    hidden = (residual_in[0].astype(jnp.float32) + projected).astype(jnp.bfloat16)
    wide = hidden.astype(jnp.float32)
    normed = (
        wide
        * lax.rsqrt(jnp.mean(wide * wide, axis=1, keepdims=True) + 1e-06)
        * norm_gain.astype(jnp.float32)
    ).astype(jnp.bfloat16)
    topk = expert_ids.shape[2]
    experts = n_seq * n_sub
    cap = max(2, (5 * tokens * topk + 4 * experts - 1) // (4 * experts))
    flat_ids = expert_ids[0].reshape(-1)
    items = flat_ids.shape[0]
    ranks = rank_in_expert(flat_ids, experts)
    slot_of = flat_ids * cap + ranks
    slots_out = experts * cap
    item_of_slot = (
        jnp.full((slots_out,), items, jnp.int32).at[slot_of].set(jnp.arange(items, dtype=jnp.int32))
    )
    padded_rows = jnp.concatenate([normed, jnp.zeros((1, D), jnp.bfloat16)], axis=0)
    padded_gates = jnp.concatenate(
        [gate_weights[0].reshape(-1), jnp.zeros((1,), jnp.bfloat16)], axis=0
    )
    token_of_slot = jnp.where(item_of_slot < items, item_of_slot // topk, tokens)
    send_rows = padded_rows[token_of_slot].reshape(experts, cap, D)
    send_gates = padded_gates[item_of_slot].reshape(experts, cap)
    recv_rows, recv_gates = (
        lax.all_to_all(send_rows, ("seq", "sub"), split_axis=0, concat_axis=0, tiled=True),
        lax.all_to_all(send_gates, ("seq", "sub"), split_axis=0, concat_axis=0, tiled=True),
    )
    slots_in = experts * cap
    valid = recv_gates > 0
    counts = jnp.sum(valid.astype(jnp.int32), axis=1)
    offsets = jnp.cumsum(counts) - counts
    dest = jnp.where(
        valid, offsets[:, None] + jnp.arange(cap, dtype=jnp.int32)[None, :], slots_in
    ).reshape(-1)
    source_of = (
        jnp.full((slots_in + 1,), slots_in, jnp.int32)
        .at[dest]
        .set(jnp.arange(slots_in, dtype=jnp.int32))[:slots_in]
    )
    compact_rows = jnp.concatenate(
        [recv_rows.reshape(slots_in, D), jnp.zeros((1, D), jnp.bfloat16)], axis=0
    )[source_of]
    compact_gates = jnp.concatenate(
        [recv_gates.reshape(-1), jnp.zeros((1,), jnp.bfloat16)], axis=0
    )[source_of].astype(jnp.float32)
    filled = jnp.sum(counts)
    n_blocks = (filled + slots_in - 1) // slots_in
    w_gate = expert_gate[0]
    w_up = expert_up[0]
    w_down = expert_down[0]

    def expert_block(index, results):
        gate_proj = jnp.dot(compact_rows, w_gate, preferred_element_type=jnp.float32)
        up_proj = jnp.dot(compact_rows, w_up, preferred_element_type=jnp.float32)
        inner = (jax.nn.silu(gate_proj) * up_proj).astype(jnp.bfloat16)
        weighted = (
            jnp.dot(inner, w_down, preferred_element_type=jnp.float32) * compact_gates[:, None]
        )
        return weighted.astype(jnp.bfloat16)

    results = lax.fori_loop(0, n_blocks, expert_block, jnp.zeros((slots_in, D), jnp.bfloat16))
    returned = jnp.concatenate([results, jnp.zeros((1, D), jnp.bfloat16)], axis=0)[dest].reshape(
        experts, cap, D
    )
    back = lax.all_to_all(
        returned, ("seq", "sub"), split_axis=0, concat_axis=0, tiled=True
    ).reshape(slots_out, D)
    gathered = back[slot_of].reshape(tokens, topk, D).astype(jnp.float32)
    mixture = jnp.sum(gathered, axis=1)
    return (wide + mixture).astype(jnp.bfloat16)[None]


def solution(mesh):
    placed = (
        P(("grp", "sub"), "seq", None),
        P(("grp", "sub"), "seq", None),
        P(("grp", "sub"), "seq", None),
        P(("grp", "sub"), "seq", None),
        P("seq", None),
        P(),
        P(("grp", "sub"), "seq", None),
        P(("grp", "sub"), "seq", None),
        P(("seq", "sub"), None, None),
        P(("seq", "sub"), None, None),
        P(("seq", "sub"), None, None),
    )
    return jax.shard_map(
        per_device,
        mesh=mesh,
        in_specs=placed,
        out_specs=P(("grp", "sub"), "seq", None),
        check_vma=False,
    )
```

profile of v0, /device:TPU:0, one launch (start us, length us, event | category | flops | bytes accessed | tf_op | source)
XLA Modules:
  0.0 475.6 jit_solution(11727438130950992658)
XLA Ops:
  7.3 3.7 copy.33
  11.6 13.3 %reduce.9 = bf16[2048,128]{1,0:T(8,128)(2,1)} reduce(bf16[2048,1,128]{2,1,0:T(2,128)(2,1)} %bitcast.127, bf16[]{:T(256)} %broadcast.193), dimensions={1}, to_apply=%bitcast.95.reduce_sub_computation | reduce | bytes 1048578
  24.9 2.0 reshape.276
  26.9 4.3 all-to-all-start
  32.2 18.7 %all_gather.9 = bf16[1,512,256]{2,1,0:T(8,128)(2,1)} all-gather(bf16[1,128,256]{2,1,0:T(8,128)(2,1)S(1)} %copy-done.6), channel_id=1, replica_groups=mesh['grp'=2,'seq'=4,'sub'=4] {'seq'}, dimensions={1}, use_global_device_ids=true | all-gather | bytes 327680 | tf_op jit(solution)/shard_map/all_gather | solution.py:76
  50.9 8.0 %all_gather.10 = bf16[1,512,256]{2,1,0:T(8,128)(2,1)S(1)} all-gather(bf16[1,128,256]{2,1,0:T(8,128)(2,1)S(1)} %copy-done.7), channel_id=1, replica_groups=mesh['grp'=2,'seq'=4,'sub'=4] {'seq'}, dimensions={1}, use_global_device_ids=true | all-gather | bytes 327680 | tf_op jit(solution)/shard_map/all_gather | solution.py:77
  58.9 3.5 reshape.277
  62.4 2.1 copy.42
  64.5 2.1 copy.34
  66.6 1.3 fusion.62
  68.1 1.3 fusion.63
  69.6 1.3 fusion.64
  71.1 1.2 fusion.65
  73.9 0.8 maximum_bitcast_fusion
  74.7 3.6 copy.35
  78.3 5.5 %reduce.10 = bf16[512,512]{1,0:T(8,128)(2,1)} reduce(bf16[512,1,512]{2,1,0:T(2,128)(2,1)} %bitcast.126, bf16[]{:T(256)} %broadcast.193), dimensions={1}, to_apply=%bitcast.97.reduce_sub_computation | reduce | bytes 1048578
  83.9 2.3 reshape.278
  86.1 4.1 all-to-all-start.1
  90.3 4.3 scatter_custom_fusion
  94.7 8.0 %gather_fusion = bf16[1280]{0:T(1024)(128)(2,1)S(1)} fusion(bf16[1025]{0:T(1024)(128)(2,1)S(1)} %pad_maximum_fusion, s32[2048]{0:T(1024)S(1)} %get-tuple-element.173), kind=kCustom, calls=%fused_computation | custom fusion | bytes 10240 | tf_op jit(solution)/shard_map/gather | solution.py:125
  103.4 7.5 %all-to-all-start.2 = ((bf16[16,1,80]{2,1,0:T(2,128)(2,1)}), bf16[16,1,80]{2,1,0:T(2,128)(2,1)S(1)}, u32[]{:S(2)}, u32[]{:S(2)}) async-start(bf16[16,1,80]{2,1,0:T(2,128)(2,1)} %all_to_all.47), calls=%async_computation.2 | async-start | bytes 16384 | tf_op jit(solution)/shard_map/all_to_all | solution.py:128
  110.9 3.5 reshape.279
  114.4 2.1 copy.43
  116.5 2.1 copy.36
  118.6 4.9 %multiply_reduce_fusion = (f32[128]{0:T(128)S(1)}, f32[128,2048]{1,0:T(8,128)S(1)}) fusion(bf16[128,2048]{0,1:T(8,128)(2,1)} %bitcast.128, bf16[2048,2048]{1,0:T(8,128)(2,1)} %all-gather.2.cloned.1.call-done, bf16[1,128,2048]{2,1,0:T(8,128)(2,1)} %param.16), kind=kOutput, calls=%fused_computation.42 | convolution fusion | flops 1075314560 | bytes 10486272 | tf_op jit(solution)/shard_map/dot_general | solution.py:96
  123.6 1.0 copy-done.2
  124.7 0.9 concatenate.21
  125.6 11.9 %gather_fusion.2 = bf16[1280,2048]{1,0:T(8,128)(2,1)} fusion(bf16[129,2048]{1,0:T(8,128)(2,1)} %concatenate.21, s32[2048]{0:T(1024)S(1)} %get-tuple-element.172), kind=kCustom, calls=%fused_computation.2 | custom fusion | bytes 10490880 | tf_op jit(solution)/shard_map/gather | solution.py:124
  137.5 6.1 %all-to-all-start.3 = ((bf16[16,80,2048]{2,1,0:T(8,128)(2,1)}), bf16[16,80,2048]{2,1,0:T(8,128)(2,1)}, u32[]{:S(2)}, u32[]{:S(2)}) async-start(bf16[16,80,2048]{2,1,0:T(8,128)(2,1)} %bitcast.122), calls=%async_computation.3 | async-start | bytes 10485760 | tf_op jit(solution)/shard_map/all_to_all | solution.py:127
  143.7 0.9 fusion.48
  146.0 5.4 %scatter_custom_fusion.1 = s32[1281]{0:T(1024)S(1)} fusion(s32[1280]{0:T(1024)S(1)} %fusion.47, s32[1280]{0:T(1024)S(1)} %iota.44, s32[]{:T(128)} %constant.125.clone.1), kind=kCustom, calls=%fused_computation.109 | custom fusion | bytes 5128 | tf_op jit(solution)/shard_map/scatter | solution.py:140
  151.5 8.0 %gather_fusion.1 = bf16[1280]{0:T(1024)(128)(2,1)S(1)} fusion(bf16[1281]{0:T(1024)(128)(2,1)S(1)} %pad_maximum_fusion.1, s32[2048]{0:T(1024)S(1)} %pad_clamp_fusion.2), kind=kCustom, calls=%fused_computation.1 | custom fusion | bytes 10240 | tf_op jit(solution)/shard_map/gather | solution.py:145
  159.5 101.0 %all-to-all-done.3 = bf16[16,80,2048]{2,1,0:T(8,128)(2,1)} async-done(((bf16[16,80,2048]{2,1,0:T(8,128)(2,1)}), bf16[16,80,2048]{2,1,0:T(8,128)(2,1)}, u32[]{:S(2)}, u32[]{:S(2)}) %all-to-all-start.3) | async-done | bytes 5242912 | tf_op jit(solution)/shard_map/all_to_all | solution.py:127
  260.5 5.7 %concatenate.22 = bf16[1281,2048]{1,0:T(8,128)(2,1)} pad(bf16[1280,2048]{1,0:T(8,128)(2,1)} %bitcast.28, bf16[]{:T(256)} %constant.121.clone.1), padding=0_1x0_0 | pad | bytes 10489858 | tf_op jit(solution)/shard_map/concatenate | solution.py:142
  266.1 14.0 %gather_fusion.3 = bf16[1280,2048]{1,0:T(8,128)(2,1)} fusion(bf16[1281,2048]{1,0:T(8,128)(2,1)} %concatenate.22, s32[2048]{0:T(1024)S(1)} %pad_clamp_fusion.2), kind=kCustom, calls=%fused_computation.3 | custom fusion | bytes 10490880 | tf_op jit(solution)/shard_map/gather | solution.py:142
  280.1 7.2 %fusion.4 = f32[1280,768]{1,0:T(8,128)S(1)} fusion(bf16[1280,2048]{1,0:T(8,128)(2,1)} %gather_fusion.3, bf16[1,2048,768]{2,1,0:T(8,128)(2,1)} %param.21), kind=kOutput, calls=%fused_computation.15 | convolution fusion | flops 4026531840 | bytes 12320768 | tf_op jit(solution)/shard_map/while/body/dot_general | solution.py:155
  287.4 4.8 %fusion = bf16[1280,768]{1,0:T(8,128)(2,1)S(1)} fusion(bf16[1280,2048]{1,0:T(8,128)(2,1)S(1)} %copy-done.4, f32[1280,768]{1,0:T(8,128)S(1)} %fusion.4, bf16[1,2048,768]{2,1,0:T(8,128)(2,1)S(1)} %copy-done.11), kind=kOutput, calls=%fused_computation.11 | convolution fusion | flops 4032430080 | bytes 14286848 | tf_op jit(solution)/shard_map/while/body/dot_general | solution.py:156
  292.2 6.9 %fusion.1 = f32[1280,2048]{1,0:T(8,128)} fusion(bf16[1280,768]{1,0:T(8,128)(2,1)S(1)} %fusion, bf16[1,768,2048]{2,1,0:T(8,128)(2,1)S(1)} %copy-done), kind=kOutput, calls=%fused_computation.12 | convolution fusion | flops 4026531840 | bytes 15597568 | tf_op jit(solution)/shard_map/while/body/dot_general | solution.py:159
  299.1 3.0 broadcast_in_dim.30
  302.1 7.1 %while.14 = (s32[]{:T(128)}, bf16[1280,2048]{1,0:T(8,128)(2,1)}, s32[]{:T(128)}, f32[1280]{0:T(1024)S(1)}, f32[1280,2048]{1,0:T(8,128)}, /*index=5*/s32[]{:T(128)}) while((s32[]{:T(128)}, bf16[1280,2048]{1,0:T(8,128)(2,1)}, s32[]{:T(128)}, f32[1280]{0:T(1024)S(1)}, f32[1280,2048]{1,0:T(8,128)}, /*index=5*/s32[]{:T(128)}) %tuple.40), condition=%wide.region_18.19_spmd, body=%wide.region_17.18_spmd.sunk | while | flops 5242882 | bytes 15733829 | solution.py:163
  302.1 7.0 %multiply_convert_fusion.3 = bf16[1280,2048]{1,0:T(8,128)(2,1)} fusion(f32[1280,2048]{1,0:T(8,128)} %get-tuple-element.220, f32[1280]{0:T(1024)S(1)} %get-tuple-element.219), kind=kLoop, calls=%fused_computation.8.clone.1 | loop fusion | flops 5242880 | bytes 15733760 | tf_op jit(solution)/shard_map/while/body/convert_element_type | solution.py:161
  309.3 5.7 %concatenate.23 = bf16[1281,2048]{1,0:T(8,128)(2,1)} pad(bf16[1280,2048]{1,0:T(8,128)(2,1)} %get-tuple-element.147, bf16[]{:T(256)} %constant.121.clone.1), padding=0_1x0_0 | pad | bytes 10489858 | tf_op jit(solution)/shard_map/concatenate | solution.py:164
  314.9 14.0 %gather_fusion.4 = bf16[1280,2048]{1,0:T(8,128)(2,1)} fusion(bf16[1281,2048]{1,0:T(8,128)(2,1)} %concatenate.23, s32[2048]{0:T(1024)S(1)} %pad_clamp_fusion), kind=kCustom, calls=%fused_computation.4 | custom fusion | bytes 10490880 | tf_op jit(solution)/shard_map/gather | solution.py:164
  328.9 4.6 all-to-all-start.4
  333.5 116.7 %all-to-all-done.4 = bf16[16,80,2048]{2,1,0:T(8,128)(2,1)} async-done(((bf16[16,80,2048]{2,1,0:T(8,128)(2,1)}), bf16[16,80,2048]{2,1,0:T(8,128)(2,1)}, u32[]{:S(2)}, u32[]{:S(2)}) %all-to-all-start.4) | async-done | bytes 5242912 | tf_op jit(solution)/shard_map/all_to_all | solution.py:167
  450.3 12.2 %gather_fusion.5 = bf16[1024,2048]{1,0:T(8,128)(2,1)} fusion(bf16[1280,2048]{1,0:T(8,128)(2,1)} %bitcast.33, s32[1024]{0:T(1024)S(1)} %broadcast_clamp_fusion), kind=kCustom, calls=%fused_computation.5 | custom fusion | bytes 8392704 | tf_op jit(solution)/shard_map/gather | solution.py:170
  462.5 5.1 %convert_reduce_fusion = f32[128,2048]{1,0:T(8,128)S(1)} fusion(bf16[1024,2048]{1,0:T(8,128)(2,1)} %gather_fusion.5), kind=kLoop, calls=%fused_computation.9 | loop fusion | flops 3932160 | bytes 5242880 | tf_op jit(solution)/shard_map/reduce_sum | solution.py:171
  467.6 0.9 fusion.23
  (77 shorter events, 6.1 us)
Async XLA Ops:
  6.5 285.7 %copy-start = (bf16[1,768,2048]{2,1,0:T(8,128)(2,1)S(1)}, bf16[1,768,2048]{2,1,0:T(8,128)(2,1)}, u32[]{:S(2)}) copy-start(bf16[1,768,2048]{2,1,0:T(8,128)(2,1)} %param.23) | copy-start | bytes 9437188
  6.5 24.6 %copy-start.10 = (bf16[1,128,8]{1,2,0:T(8,128)(2,1)S(1)}, bf16[1,128,8]{1,2,0:T(8,128)(2,1)}, u32[]{:S(2)}) copy-start(bf16[1,128,8]{1,2,0:T(8,128)(2,1)} %param.20) | copy-start | bytes 6148
  6.5 24.9 %copy-start.8 = (s32[1,128,8]{1,2,0:T(8,128)S(1)}, s32[1,128,8]{1,2,0:T(8,128)}, u32[]{:S(2)}) copy-start(s32[1,128,8]{1,2,0:T(8,128)} %param.19) | copy-start | bytes 12292
  6.5 25.6 %copy-start.6 = (bf16[1,128,256]{2,1,0:T(8,128)(2,1)S(1)}, bf16[1,128,256]{2,1,0:T(8,128)(2,1)}, u32[]{:S(2)}) copy-start(bf16[1,128,256]{2,1,0:T(8,128)(2,1)} %param.14) | copy-start | bytes 196612
  6.5 44.3 %copy-start.7 = (bf16[1,128,256]{2,1,0:T(8,128)(2,1)S(1)}, bf16[1,128,256]{2,1,0:T(8,128)(2,1)}, u32[]{:S(2)}) copy-start(bf16[1,128,256]{2,1,0:T(8,128)(2,1)} %param.15) | copy-start | bytes 196612
  6.5 112.0 %all-gather.2.cloned.1.call-start = ((), (), s32[]{:S(2)}) async-start(), calls=%async_computation.5 | async-start | bytes 10485760 | tf_op jit(solution)/shard_map/all_gather | solution.py:98
  26.9 32.0 %all-to-all-start = ((bf16[4,2,32768]{2,1,0:T(2,128)(2,1)}), bf16[4,2,32768]{2,1,0:T(2,128)(2,1)}, u32[]{:S(2)}, u32[]{:S(2)}) async-start(bf16[4,2,32768]{2,1,0:T(2,128)(2,1)} %reshape.276), calls=%async_computation | async-start | bytes 1048576 | tf_op jit(solution)/shard_map/all_to_all | solution.py:74
  66.6 4.5 copy-start.5
  73.5 16.8 %copy-start.9 = (bf16[2048]{0:T(1024)(128)(2,1)S(1)}, bf16[2048]{0:T(1024)(128)(2,1)}, u32[]{:S(2)}) copy-start(bf16[2048]{0:T(1024)(128)(2,1)} %param.18) | copy-start | bytes 12292
  86.1 17.2 %all-to-all-start.1 = ((bf16[4,2,32768]{2,1,0:T(2,128)(2,1)}), bf16[4,2,32768]{2,1,0:T(2,128)(2,1)}, u32[]{:S(2)}, u32[]{:S(2)}) async-start(bf16[4,2,32768]{2,1,0:T(2,128)(2,1)} %reshape.278), calls=%async_computation.1 | async-start | bytes 1048576 | tf_op jit(solution)/shard_map/all_to_all | solution.py:95
  103.4 34.2 %all-to-all-start.2 = ((bf16[16,1,80]{2,1,0:T(2,128)(2,1)}), bf16[16,1,80]{2,1,0:T(2,128)(2,1)S(1)}, u32[]{:S(2)}, u32[]{:S(2)}) async-start(bf16[16,1,80]{2,1,0:T(2,128)(2,1)} %all_to_all.47), calls=%async_computation.2 | async-start | bytes 16384 | tf_op jit(solution)/shard_map/all_to_all | solution.py:128
  123.5 1.0 copy-start.2
  137.5 122.9 %all-to-all-start.3 = ((bf16[16,80,2048]{2,1,0:T(8,128)(2,1)}), bf16[16,80,2048]{2,1,0:T(8,128)(2,1)}, u32[]{:S(2)}, u32[]{:S(2)}) async-start(bf16[16,80,2048]{2,1,0:T(8,128)(2,1)} %bitcast.122), calls=%async_computation.3 | async-start | bytes 10485760 | tf_op jit(solution)/shard_map/all_to_all | solution.py:127
  280.1 7.3 %copy-start.4 = (bf16[1280,2048]{1,0:T(8,128)(2,1)S(1)}, bf16[1280,2048]{1,0:T(8,128)(2,1)}, u32[]{:S(2)}) copy-start(bf16[1280,2048]{1,0:T(8,128)(2,1)} %gather_fusion.3) | copy-start | bytes 15728644
  280.1 7.3 %copy-start.11 = (bf16[1,2048,768]{2,1,0:T(8,128)(2,1)S(1)}, bf16[1,2048,768]{2,1,0:T(8,128)(2,1)}, u32[]{:S(2)}) copy-start(bf16[1,2048,768]{2,1,0:T(8,128)(2,1)} %param.22) | copy-start | bytes 9437188
  328.9 121.3 %all-to-all-start.4 = ((bf16[16,80,2048]{2,1,0:T(8,128)(2,1)}), bf16[16,80,2048]{2,1,0:T(8,128)(2,1)}, u32[]{:S(2)}, u32[]{:S(2)}) async-start(bf16[16,80,2048]{2,1,0:T(8,128)(2,1)} %bitcast.123), calls=%async_computation.4 | async-start | bytes 10485760 | tf_op jit(solution)/shard_map/all_to_all | solution.py:167
  450.3 18.3 %copy-start.1 = (bf16[1,768,2048]{2,1,0:T(8,128)(2,1)S(1)}, bf16[1,768,2048]{2,1,0:T(8,128)(2,1)}, u32[]{:S(2)}) copy-start(bf16[1,768,2048]{2,1,0:T(8,128)(2,1)} %param.23) | copy-start | bytes 9437188
  462.5 5.1 %copy-start.3 = (f32[128,2048]{1,0:T(8,128)S(1)}, f32[128,2048]{1,0:T(8,128)}, u32[]{:S(2)}) copy-start(f32[128,2048]{1,0:T(8,128)} %copy-done.2) | copy-start | bytes 3145732
Sparse Core Ops, SparseCore 0:
  8.9 69.4 all-gather.1
where the time goes:
time: 482 us; the launch traced here: 476 us
  waiting for transfers between devices  218 us (45%)
  local copies, waits for them, and re-layouts  123 us (26%)
  other arithmetic  35.1 us (7%)
  matrix products  30.5 us (6%)
  blocking collectives  26.7 us (6%)
  starting transfers between devices  26.6 us (6%)
  between operations  14.7 us (3%)
    all_to_all x1, waiting for transfers between devices, per_device(): lax.all_to_all(returned, ('seq', 'sub'), split_axis=0, concat_axis=0, til...  117 us
    all_to_all x1, waiting for transfers between devices, per_device(): lax.all_to_all(send_rows, ('seq', 'sub'), split_axis=0, concat_axis=0, ti...  101 us
    unnamed x34, local copies, waits for them, and re-layouts  21.1 us
    unnamed x2, other arithmetic  18.9 us
    all_gather x1, blocking collectives, per_device(): lax.all_gather(key_rows, 'seq', axis=1, tiled=True)  18.7 us
    gather x1, local copies, waits for them, and re-layouts, per_device(): jnp.concatenate([recv_rows.reshape(slots_in, D), jnp.zeros((1, D), jnp.bf...  14 us
    gather x1, local copies, waits for them, and re-layouts, per_device(): jnp.concatenate([results, jnp.zeros((1, D), jnp.bfloat16)], axis=0)[dest]  14 us
    gather x1, local copies, waits for them, and re-layouts, per_device(): gathered = back[slot_of].reshape(tokens, topk, D).astype(jnp.float32)  12.2 us
  transfers between devices with their start and end apart: 6, of which 2 were waited for; matrix products, arithmetic and copies ran while one was open for 21% of the time, Pallas kernels for 0%

commit v1 on v0

--- a/solution.py
+++ b/solution.py
@@ -7,6 +7,30 @@
 HD = 128
 QH = 16
 KVH = 2
+
+
+def in_blocks(x, dim, peers):
+    shape = x.shape
+    parts = x.reshape(*shape[:dim], peers, shape[dim] // peers, *shape[dim + 1 :])
+    return jnp.moveaxis(parts, dim, 0)
+
+
+def laid_out(blocks, dim):
+    blocks = jnp.moveaxis(blocks, 0, dim)
+    lengths = blocks.shape
+    return blocks.reshape(*lengths[:dim], lengths[dim] * lengths[dim + 1], *lengths[dim + 2 :])
+
+
+def exchange_directly(x, axis, split_dim, concat_dim):
+    peers, index = (lax.axis_size(axis), lax.axis_index(axis))
+    parts = in_blocks(x, split_dim, peers)
+    out = parts
+    for lap in range(1, peers):
+        target, source = ((index + lap) % peers, (index - lap) % peers)
+        sent = lax.dynamic_index_in_dim(parts, target, 0)
+        other = lax.ppermute(sent, axis, [(i, (i + lap) % peers) for i in range(peers)])
+        out = lax.dynamic_update_slice_in_dim(out, other, source, axis=0)
+    return laid_out(out, concat_dim)
 
 
 def attend_head(queries, keys_one, values_one, block):
@@ -124,7 +148,7 @@
     send_rows = padded_rows[token_of_slot].reshape(experts, cap, D)
     send_gates = padded_gates[item_of_slot].reshape(experts, cap)
     recv_rows, recv_gates = (
-        lax.all_to_all(send_rows, ("seq", "sub"), split_axis=0, concat_axis=0, tiled=True),
+        exchange_directly(send_rows, ("seq", "sub"), 0, 0),
         lax.all_to_all(send_gates, ("seq", "sub"), split_axis=0, concat_axis=0, tiled=True),
     )
     slots_in = experts * cap

time: 482 us -> 506 us (1.050)
  starting transfers between devices: 26.6 us -> 71.4 us
  waiting for transfers between devices: 218 us -> 188 us
  local copies, waits for them, and re-layouts: 123 us -> 140 us
  blocking collectives: 26.7 us -> 17 us
    all_to_all x1 -> x0, waiting for transfers between devices: 101 us -> none  [per_device(): lax.all_to_all(send_rows, ('seq', 'sub'), split_axis=0, concat_axis=0, ti...]
    ppermute x0 -> x15, waiting for transfers between devices: none -> 64.4 us  [exchange_directly(): lax.ppermute(sent, axis, [(i, (i + lap) % peers) for i in range(peers)])]
    ppermute x0 -> x15, starting transfers between devices: none -> 45.5 us  [exchange_directly(): lax.ppermute(sent, axis, [(i, (i + lap) % peers) for i in range(peers)])]
    dynamic_update_slice x0 -> x14, local copies, waits for them, and re-layouts: none -> 11.6 us  [exchange_directly(): out = lax.dynamic_update_slice_in_dim(out, other, source, axis=0)]
    all_gather x1, blocking collectives: 18.7 us -> 9.25 us  [per_device(): lax.all_gather(key_rows, 'seq', axis=1, tiled=True)]
    all_to_all x1, waiting for transfers between devices: 0.01 us -> 6.6 us  [per_device(): lax.all_to_all(head_block, 'seq', split_axis=1, concat_axis=2, tiled=True)]
    all_to_all x1, starting transfers between devices: 4.57 us -> 10.9 us  [per_device(): lax.all_to_all(returned, ('seq', 'sub'), split_axis=0, concat_axis=0, til...]
    all_to_all x1 -> x0, starting transfers between devices: 6.15 us -> none  [per_device(): lax.all_to_all(send_rows, ('seq', 'sub'), split_axis=0, concat_axis=0, ti...]
  transfers between devices with their start and end apart: 6 -> 20, of which waited for: 2 -> 11; matrix products, arithmetic and copies ran while one was open for 21% -> 19% of each run, Pallas kernels for 0% -> 0%
where the time goes in v1:
time: 506 us; the launch traced here: 498 us
  waiting for transfers between devices  188 us (37%)
  local copies, waits for them, and re-layouts  140 us (28%)
  starting transfers between devices  71.4 us (14%)
  other arithmetic  35.1 us (7%)
  matrix products  30.6 us (6%)
  blocking collectives  17 us (3%)
  between operations  15.1 us (3%)
    all_to_all x1, waiting for transfers between devices, per_device(): lax.all_to_all(returned, ('seq', 'sub'), split_axis=0, concat_axis=0, til...  117 us
    ppermute x15, waiting for transfers between devices, exchange_directly(): lax.ppermute(sent, axis, [(i, (i + lap) % peers) for i in range(peers)])  64.4 us
    ppermute x15, starting transfers between devices, exchange_directly(): lax.ppermute(sent, axis, [(i, (i + lap) % peers) for i in range(peers)])  45.5 us
    unnamed x36, local copies, waits for them, and re-layouts  21 us
    unnamed x2, other arithmetic  18.9 us
    gather x1, local copies, waits for them, and re-layouts, per_device(): jnp.concatenate([recv_rows.reshape(slots_in, D), jnp.zeros((1, D), jnp.bf...  14 us
    gather x1, local copies, waits for them, and re-layouts, per_device(): jnp.concatenate([results, jnp.zeros((1, D), jnp.bfloat16)], axis=0)[dest]  14 us
    gather x1, local copies, waits for them, and re-layouts, per_device(): gathered = back[slot_of].reshape(tokens, topk, D).astype(jnp.float32)  12.2 us
  transfers between devices with their start and end apart: 20, of which 11 were waited for; matrix products, arithmetic and copies ran while one was open for 19% of the time, Pallas kernels for 0%

profile of v1, /device:TPU:0, one launch (start us, length us, event | category | flops | bytes accessed | tf_op | source)
XLA Modules:
  0.0 498.0 jit_solution(7794672840865573303)
XLA Ops:
  7.3 3.7 copy.33
  11.5 13.3 %reduce.9 = bf16[2048,128]{1,0:T(8,128)(2,1)} reduce(bf16[2048,1,128]{2,1,0:T(2,128)(2,1)} %bitcast.129, bf16[]{:T(256)} %broadcast.223), dimensions={1}, to_apply=%bitcast.95.reduce_sub_computation | reduce | bytes 1048578
  26.9 4.3 all-to-all-start
  32.6 4.3 scatter_custom_fusion
  36.9 8.0 %gather_fusion = bf16[1280]{0:T(1024)(128)(2,1)S(1)} fusion(bf16[1025]{0:T(1024)(128)(2,1)S(1)} %pad_maximum_fusion, s32[2048]{0:T(1024)S(1)} %get-tuple-element.188), kind=kCustom, calls=%fused_computation | custom fusion | bytes 10240 | tf_op jit(solution)/shard_map/gather | solution.py:149
  45.6 9.3 %all_gather.9 = bf16[1,512,256]{2,1,0:T(8,128)(2,1)} all-gather(bf16[1,128,256]{2,1,0:T(8,128)(2,1)S(1)} %copy-done.7), channel_id=1, replica_groups=mesh['grp'=2,'seq'=4,'sub'=4] {'seq'}, dimensions={1}, use_global_device_ids=true | all-gather | bytes 327680 | tf_op jit(solution)/shard_map/all_gather | solution.py:100
  54.9 7.7 %all_gather.10 = bf16[1,512,256]{2,1,0:T(8,128)(2,1)S(1)} all-gather(bf16[1,128,256]{2,1,0:T(8,128)(2,1)S(1)} %copy-done.8), channel_id=1, replica_groups=mesh['grp'=2,'seq'=4,'sub'=4] {'seq'}, dimensions={1}, use_global_device_ids=true | all-gather | bytes 327680 | tf_op jit(solution)/shard_map/all_gather | solution.py:101
  62.6 6.6 %all-to-all-start.2 = ((bf16[16,1,80]{2,1,0:T(2,128)(2,1)}), bf16[16,1,80]{2,1,0:T(2,128)(2,1)S(1)}, u32[]{:S(2)}, u32[]{:S(2)}) async-start(bf16[16,1,80]{2,1,0:T(2,128)(2,1)} %all_to_all.43), calls=%async_computation.2 | async-start | bytes 16384 | tf_op jit(solution)/shard_map/all_to_all | solution.py:152
  69.2 3.5 reshape.269
  85.1 3.6 copy.35
  88.7 5.5 %reduce.10 = bf16[512,512]{1,0:T(8,128)(2,1)} reduce(bf16[512,1,512]{2,1,0:T(2,128)(2,1)} %bitcast.128, bf16[]{:T(256)} %broadcast.223), dimensions={1}, to_apply=%bitcast.97.reduce_sub_computation | reduce | bytes 1048578
  96.5 4.1 all-to-all-start.1
  102.9 6.6 %all-to-all-done.1 = bf16[4,2,32768]{2,1,0:T(2,128)(2,1)} async-done(((bf16[4,2,32768]{2,1,0:T(2,128)(2,1)}), bf16[4,2,32768]{2,1,0:T(2,128)(2,1)}, u32[]{:S(2)}, u32[]{:S(2)}) %all-to-all-start.1) | async-done | bytes 524320 | tf_op jit(solution)/shard_map/all_to_all | solution.py:119
  109.5 3.5 reshape.271
  117.3 4.9 multiply_reduce_fusion
  124.2 11.9 %gather_fusion.2 = bf16[1280,2048]{1,0:T(8,128)(2,1)} fusion(bf16[129,2048]{1,0:T(8,128)(2,1)} %concatenate.21, s32[2048]{0:T(1024)S(1)} %get-tuple-element.187), kind=kCustom, calls=%fused_computation.2 | custom fusion | bytes 10490880 | tf_op jit(solution)/shard_map/gather | solution.py:148
  139.5 5.2 %scatter_custom_fusion.1 = s32[1281]{0:T(1024)S(1)} fusion(s32[1280]{0:T(1024)S(1)} %fusion.55, s32[1280]{0:T(1024)S(1)} %iota.44, s32[]{:T(128)} %constant.310.clone.1), kind=kCustom, calls=%fused_computation.147 | custom fusion | bytes 5128 | tf_op jit(solution)/shard_map/scatter | solution.py:164
  144.7 5.0 %collective-permute-done = bf16[1,1,80,2048]{3,2,0,1:T(8,128)(2,1)} collective-permute-done((bf16[1,1,80,2048]{3,2,0,1:T(8,128)(2,1)S(1)}, bf16[1,1,80,2048]{3,2,0,1:T(8,128)(2,1)}, u32[]{:S(2)}, u32[]{:S(2)}) %collective-permute-start) | collective-permute-done | bytes 327712 | tf_op jit(solution)/shard_map/ppermute | solution.py:31
  149.7 4.5 constant_dynamic-slice_fusion
  154.3 8.0 %gather_fusion.1 = bf16[1280]{0:T(1024)(128)(2,1)S(1)} fusion(bf16[1281]{0:T(1024)(128)(2,1)S(1)} %pad_maximum_fusion.1, s32[2048]{0:T(1024)S(1)} %pad_clamp_fusion.2), kind=kCustom, calls=%fused_computation.1 | custom fusion | bytes 10240 | tf_op jit(solution)/shard_map/gather | solution.py:169
  163.2 3.4 collective-permute-start.14
  167.7 3.6 collective-permute-done.1
  173.0 5.1 %collective-permute-done.2 = bf16[1,1,80,2048]{3,2,0,1:T(8,128)(2,1)S(1)} collective-permute-done((bf16[1,1,80,2048]{3,2,0,1:T(8,128)(2,1)}, bf16[1,1,80,2048]{3,2,0,1:T(8,128)(2,1)S(1)}, u32[]{:S(2)}, u32[]{:S(2)}) %collective-permute-start.2) | collective-permute-done | bytes 327712 | tf_op jit(solution)/shard_map/ppermute | solution.py:31
  178.2 15.2 %collective-permute-start.4 = (bf16[1,1,80,2048]{3,2,0,1:T(8,128)(2,1)}, bf16[1,1,80,2048]{3,2,0,1:T(8,128)(2,1)S(1)}, u32[]{:S(2)}, u32[]{:S(2)}) collective-permute-start(bf16[1,1,80,2048]{3,2,0,1:T(8,128)(2,1)} %get-tuple-element.170), channel_id=1, source_target_pairs={{0,5},{1,6},{2,7},{3,8},{4,9},{5,10},{6,11},{7,12},{8,13},{9,14},{... | collective-permute-start | bytes 983048 | tf_op jit(solution)/shard_map/ppermute | solution.py:31
  194.1 2.9 collective-permute-start.5
  197.7 6.3 %collective-permute-done.4 = bf16[1,1,80,2048]{3,2,0,1:T(8,128)(2,1)S(1)} collective-permute-done((bf16[1,1,80,2048]{3,2,0,1:T(8,128)(2,1)}, bf16[1,1,80,2048]{3,2,0,1:T(8,128)(2,1)S(1)}, u32[]{:S(2)}, u32[]{:S(2)}) %collective-permute-start.4) | collective-permute-done | bytes 327712 | tf_op jit(solution)/shard_map/ppermute | solution.py:31
  204.0 2.8 collective-permute-start.6
  207.6 19.7 %collective-permute-done.5 = bf16[1,1,80,2048]{3,2,0,1:T(8,128)(2,1)S(1)} collective-permute-done((bf16[1,1,80,2048]{3,2,0,1:T(8,128)(2,1)}, bf16[1,1,80,2048]{3,2,0,1:T(8,128)(2,1)S(1)}, u32[]{:S(2)}, u32[]{:S(2)}) %collective-permute-start.5) | collective-permute-done | bytes 327712 | tf_op jit(solution)/shard_map/ppermute | solution.py:31
  229.4 5.0 %collective-permute-done.6 = bf16[1,1,80,2048]{3,2,0,1:T(8,128)(2,1)S(1)} collective-permute-done((bf16[1,1,80,2048]{3,2,0,1:T(8,128)(2,1)}, bf16[1,1,80,2048]{3,2,0,1:T(8,128)(2,1)S(1)}, u32[]{:S(2)}, u32[]{:S(2)}) %collective-permute-start.6) | collective-permute-done | bytes 327712 | tf_op jit(solution)/shard_map/ppermute | solution.py:31
  234.4 3.3 collective-permute-start.8
  238.5 5.0 %collective-permute-done.7 = bf16[1,1,80,2048]{3,2,0,1:T(8,128)(2,1)S(1)} collective-permute-done((bf16[1,1,80,2048]{3,2,0,1:T(8,128)(2,1)}, bf16[1,1,80,2048]{3,2,0,1:T(8,128)(2,1)S(1)}, u32[]{:S(2)}, u32[]{:S(2)}) %collective-permute-start.7) | collective-permute-done | bytes 327712 | tf_op jit(solution)/shard_map/ppermute | solution.py:31
  243.5 8.5 %collective-permute-start.9 = (bf16[1,1,80,2048]{3,2,0,1:T(8,128)(2,1)}, bf16[1,1,80,2048]{3,2,0,1:T(8,128)(2,1)S(1)}, u32[]{:S(2)}, u32[]{:S(2)}) collective-permute-start(bf16[1,1,80,2048]{3,2,0,1:T(8,128)(2,1)} %get-tuple-element.165), channel_id=1, source_target_pairs={{0,10},{1,11},{2,12},{3,13},{4,14},{5,15},{6,0},{7,1},{8,2},{9,3},... | collective-permute-start | bytes 983048 | tf_op jit(solution)/shard_map/ppermute | solution.py:31
  255.1 11.6 %collective-permute-done.9 = bf16[1,1,80,2048]{3,2,0,1:T(8,128)(2,1)S(1)} collective-permute-done((bf16[1,1,80,2048]{3,2,0,1:T(8,128)(2,1)}, bf16[1,1,80,2048]{3,2,0,1:T(8,128)(2,1)S(1)}, u32[]{:S(2)}, u32[]{:S(2)}) %collective-permute-start.9) | collective-permute-done | bytes 327712 | tf_op jit(solution)/shard_map/ppermute | solution.py:31
  270.4 3.1 collective-permute-done.11
  276.5 5.7 %concatenate.22 = bf16[1281,2048]{1,0:T(8,128)(2,1)} pad(bf16[1280,2048]{1,0:T(8,128)(2,1)} %bitcast.124, bf16[]{:T(256)} %constant.306.clone.1), padding=0_1x0_0 | pad | bytes 10489858 | tf_op jit(solution)/shard_map/concatenate | solution.py:166
  282.2 14.0 %gather_fusion.3 = bf16[1280,2048]{1,0:T(8,128)(2,1)} fusion(bf16[1281,2048]{1,0:T(8,128)(2,1)} %concatenate.22, s32[2048]{0:T(1024)S(1)} %pad_clamp_fusion.2), kind=kCustom, calls=%fused_computation.3 | custom fusion | bytes 10490880 | tf_op jit(solution)/shard_map/gather | solution.py:166
  296.2 7.2 %fusion.4 = f32[1280,768]{1,0:T(8,128)S(1)} fusion(bf16[1280,2048]{1,0:T(8,128)(2,1)} %gather_fusion.3, bf16[1,2048,768]{2,1,0:T(8,128)(2,1)} %param.21), kind=kOutput, calls=%fused_computation.15 | convolution fusion | flops 4026531840 | bytes 12320768 | tf_op jit(solution)/shard_map/while/body/dot_general | solution.py:179
  303.5 4.8 fusion
  308.3 6.9 %fusion.1 = f32[1280,2048]{1,0:T(8,128)} fusion(bf16[1280,768]{1,0:T(8,128)(2,1)S(1)} %fusion, bf16[1,768,2048]{2,1,0:T(8,128)(2,1)S(1)} %copy-done), kind=kOutput, calls=%fused_computation.12 | convolution fusion | flops 4026531840 | bytes 15597568 | tf_op jit(solution)/shard_map/while/body/dot_general | solution.py:183
  315.2 3.0 broadcast_in_dim.30
  318.2 7.2 %while.14 = (s32[]{:T(128)}, bf16[1280,2048]{1,0:T(8,128)(2,1)}, s32[]{:T(128)}, f32[1280]{0:T(1024)S(1)}, f32[1280,2048]{1,0:T(8,128)}, /*index=5*/s32[]{:T(128)}) while((s32[]{:T(128)}, bf16[1280,2048]{1,0:T(8,128)(2,1)}, s32[]{:T(128)}, f32[1280]{0:T(1024)S(1)}, f32[1280,2048]{1,0:T(8,128)}, /*index=5*/s32[]{:T(128)}) %tuple.54), condition=%wide.region_18.19_spmd, body=%wide.region_17.18_spmd.sunk | while | flops 5242882 | bytes 15733829 | solution.py:187
  318.2 7.0 %multiply_convert_fusion.3 = bf16[1280,2048]{1,0:T(8,128)(2,1)} fusion(f32[1280,2048]{1,0:T(8,128)} %get-tuple-element.235, f32[1280]{0:T(1024)S(1)} %get-tuple-element.234), kind=kLoop, calls=%fused_computation.8.clone.1 | loop fusion | flops 5242880 | bytes 15733760 | tf_op jit(solution)/shard_map/while/body/convert_element_type | solution.py:185
  325.4 5.7 %concatenate.23 = bf16[1281,2048]{1,0:T(8,128)(2,1)} pad(bf16[1280,2048]{1,0:T(8,128)(2,1)} %get-tuple-element.147, bf16[]{:T(256)} %constant.306.clone.1), padding=0_1x0_0 | pad | bytes 10489858 | tf_op jit(solution)/shard_map/concatenate | solution.py:188
  331.0 14.0 %gather_fusion.4 = bf16[1280,2048]{1,0:T(8,128)(2,1)} fusion(bf16[1281,2048]{1,0:T(8,128)(2,1)} %concatenate.23, s32[2048]{0:T(1024)S(1)} %pad_clamp_fusion), kind=kCustom, calls=%fused_computation.4 | custom fusion | bytes 10490880 | tf_op jit(solution)/shard_map/gather | solution.py:188
  345.0 10.9 %all-to-all-start.3 = ((bf16[16,80,2048]{2,1,0:T(8,128)(2,1)}), bf16[16,80,2048]{2,1,0:T(8,128)(2,1)}, u32[]{:S(2)}, u32[]{:S(2)}) async-start(bf16[16,80,2048]{2,1,0:T(8,128)(2,1)} %bitcast.125), calls=%async_computation.3 | async-start | bytes 10485760 | tf_op jit(solution)/shard_map/all_to_all | solution.py:191
  355.9 116.8 %all-to-all-done.3 = bf16[16,80,2048]{2,1,0:T(8,128)(2,1)} async-done(((bf16[16,80,2048]{2,1,0:T(8,128)(2,1)}), bf16[16,80,2048]{2,1,0:T(8,128)(2,1)}, u32[]{:S(2)}, u32[]{:S(2)}) %all-to-all-start.3) | async-done | bytes 5242912 | tf_op jit(solution)/shard_map/all_to_all | solution.py:191
  472.7 12.2 %gather_fusion.5 = bf16[1024,2048]{1,0:T(8,128)(2,1)} fusion(bf16[1280,2048]{1,0:T(8,128)(2,1)} %bitcast.33, s32[1024]{0:T(1024)S(1)} %broadcast_clamp_fusion), kind=kCustom, calls=%fused_computation.5 | custom fusion | bytes 8392704 | tf_op jit(solution)/shard_map/gather | solution.py:194
  484.9 5.1 %convert_reduce_fusion = f32[128,2048]{1,0:T(8,128)S(1)} fusion(bf16[1024,2048]{1,0:T(8,128)(2,1)} %gather_fusion.5), kind=kLoop, calls=%fused_computation.9 | loop fusion | flops 3932160 | bytes 5242880 | tf_op jit(solution)/shard_map/reduce_sum | solution.py:195
  (123 shorter events, 50.4 us)
Async XLA Ops:
  6.5 301.7 %copy-start = (bf16[1,768,2048]{2,1,0:T(8,128)(2,1)S(1)}, bf16[1,768,2048]{2,1,0:T(8,128)(2,1)}, u32[]{:S(2)}) copy-start(bf16[1,768,2048]{2,1,0:T(8,128)(2,1)} %param.23) | copy-start | bytes 9437188
  6.5 25.0 %copy-start.10 = (bf16[2048]{0:T(1024)(128)(2,1)S(1)}, bf16[2048]{0:T(1024)(128)(2,1)}, u32[]{:S(2)}) copy-start(bf16[2048]{0:T(1024)(128)(2,1)} %param.18) | copy-start | bytes 12292
  6.5 25.0 %copy-start.11 = (bf16[1,128,8]{1,2,0:T(8,128)(2,1)S(1)}, bf16[1,128,8]{1,2,0:T(8,128)(2,1)}, u32[]{:S(2)}) copy-start(bf16[1,128,8]{1,2,0:T(8,128)(2,1)} %param.20) | copy-start | bytes 6148
  6.5 25.3 %copy-start.9 = (s32[1,128,8]{1,2,0:T(8,128)S(1)}, s32[1,128,8]{1,2,0:T(8,128)}, u32[]{:S(2)}) copy-start(s32[1,128,8]{1,2,0:T(8,128)} %param.19) | copy-start | bytes 12292
  6.5 110.7 %all-gather.2.cloned.1.call-start = ((), (), s32[]{:S(2)}) async-start(), calls=%async_computation.4 | async-start | bytes 10485760 | tf_op jit(solution)/shard_map/all_gather | solution.py:122
  7.3 38.3 %copy-start.7 = (bf16[1,128,256]{2,1,0:T(8,128)(2,1)S(1)}, bf16[1,128,256]{2,1,0:T(8,128)(2,1)}, u32[]{:S(2)}) copy-start(bf16[1,128,256]{2,1,0:T(8,128)(2,1)} %param.14) | copy-start | bytes 196612
  11.0 43.8 %copy-start.8 = (bf16[1,128,256]{2,1,0:T(8,128)(2,1)S(1)}, bf16[1,128,256]{2,1,0:T(8,128)(2,1)}, u32[]{:S(2)}) copy-start(bf16[1,128,256]{2,1,0:T(8,128)(2,1)} %param.15) | copy-start | bytes 196612
  26.9 35.7 %all-to-all-start = ((bf16[4,2,32768]{2,1,0:T(2,128)(2,1)}), bf16[4,2,32768]{2,1,0:T(2,128)(2,1)}, u32[]{:S(2)}, u32[]{:S(2)}) async-start(bf16[4,2,32768]{2,1,0:T(2,128)(2,1)} %reshape.268), calls=%async_computation | async-start | bytes 1048576 | tf_op jit(solution)/shard_map/all_to_all | solution.py:98
  62.6 33.9 %all-to-all-start.2 = ((bf16[16,1,80]{2,1,0:T(2,128)(2,1)}), bf16[16,1,80]{2,1,0:T(2,128)(2,1)S(1)}, u32[]{:S(2)}, u32[]{:S(2)}) async-start(bf16[16,1,80]{2,1,0:T(2,128)(2,1)} %all_to_all.43), calls=%async_computation.2 | async-start | bytes 16384 | tf_op jit(solution)/shard_map/all_to_all | solution.py:152
  76.9 4.5 copy-start.6
  96.5 13.0 %all-to-all-start.1 = ((bf16[4,2,32768]{2,1,0:T(2,128)(2,1)}), bf16[4,2,32768]{2,1,0:T(2,128)(2,1)}, u32[]{:S(2)}, u32[]{:S(2)}) async-start(bf16[4,2,32768]{2,1,0:T(2,128)(2,1)} %reshape.270), calls=%async_computation.1 | async-start | bytes 1048576 | tf_op jit(solution)/shard_map/all_to_all | solution.py:119
  122.2 1.0 copy-start.2
  137.2 12.5 %collective-permute-start = (bf16[1,1,80,2048]{3,2,0,1:T(8,128)(2,1)S(1)}, bf16[1,1,80,2048]{3,2,0,1:T(8,128)(2,1)}, u32[]{:S(2)}, u32[]{:S(2)}) collective-permute-start(bf16[1,1,80,2048]{3,2,0,1:T(8,128)(2,1)S(1)} %constant_dynamic-slice_fusion.14), channel_id=1, source_target_pairs={{0,1},{1,2},{2,3},{3,4},{4,5},{5,6},{6,7},{7,8},{8,9},{9,10},{10,1... | collective-permute-start | bytes 983048 | tf_op jit(solution)/shard_map/ppermute | solution.py:31
  154.2 17.1 %collective-permute-start.1 = (bf16[1,1,80,2048]{3,2,0,1:T(8,128)(2,1)}, bf16[1,1,80,2048]{3,2,0,1:T(8,128)(2,1)}, u32[]{:S(2)}, u32[]{:S(2)}) collective-permute-start(bf16[1,1,80,2048]{3,2,0,1:T(8,128)(2,1)} %get-tuple-element.173), channel_id=1, source_target_pairs={{0,2},{1,3},{2,4},{3,5},{4,6},{5,7},{6,8},{7,9},{8,10},{9,11},{10,... | collective-permute-start | bytes 983048 | tf_op jit(solution)/shard_map/ppermute | solution.py:31
  162.3 104.5 %copy-start.5 = (bf16[1,1,80,2048]{3,2,0,1:T(8,128)(2,1)S(1)}, bf16[1,1,80,2048]{3,2,0,1:T(8,128)(2,1)}, u32[]{:S(2)}) copy-start(bf16[1,1,80,2048]{3,2,0,1:T(8,128)(2,1)} %get-tuple-element.163) | copy-start | bytes 983044
  162.3 15.8 %collective-permute-start.2 = (bf16[1,1,80,2048]{3,2,0,1:T(8,128)(2,1)}, bf16[1,1,80,2048]{3,2,0,1:T(8,128)(2,1)S(1)}, u32[]{:S(2)}, u32[]{:S(2)}) collective-permute-start(bf16[1,1,80,2048]{3,2,0,1:T(8,128)(2,1)} %get-tuple-element.172), channel_id=1, source_target_pairs={{0,3},{1,4},{2,5},{3,6},{4,7},{5,8},{6,9},{7,10},{8,11},{9,12},{10... | collective-permute-start | bytes 983048 | tf_op jit(solution)/shard_map/ppermute | solution.py:31
  163.2 112.6 %collective-permute-start.14 = (bf16[1,1,80,2048]{3,2,0,1:T(8,128)(2,1)S(1)}, bf16[1,1,80,2048]{3,2,0,1:T(8,128)(2,1)S(1)}, u32[]{:S(2)}, u32[]{:S(2)}) collective-permute-start(bf16[1,1,80,2048]{3,2,0,1:T(8,128)(2,1)S(1)} %get-tuple-element.160), channel_id=1, source_target_pairs={{0,15},{1,0},{2,1},{3,2},{4,3},{5,4},{6,5},{7,6},{8,7},{9,8},{10,9... | collective-permute-start | bytes 983048 | tf_op jit(solution)/shard_map/ppermute | solution.py:31
  166.6 108.5 %collective-permute-start.13 = (bf16[1,1,80,2048]{3,2,0,1:T(8,128)(2,1)}, bf16[1,1,80,2048]{3,2,0,1:T(8,128)(2,1)S(1)}, u32[]{:S(2)}, u32[]{:S(2)}) collective-permute-start(bf16[1,1,80,2048]{3,2,0,1:T(8,128)(2,1)} %get-tuple-element.161), channel_id=1, source_target_pairs={{0,14},{1,15},{2,0},{3,1},{4,2},{5,3},{6,4},{7,5},{8,6},{9,7},{10,... | collective-permute-start | bytes 983048 | tf_op jit(solution)/shard_map/ppermute | solution.py:31
  166.6 107.7 %collective-permute-start.12 = (bf16[1,1,80,2048]{3,2,0,1:T(8,128)(2,1)}, bf16[1,1,80,2048]{3,2,0,1:T(8,128)(2,1)S(1)}, u32[]{:S(2)}, u32[]{:S(2)}) collective-permute-start(bf16[1,1,80,2048]{3,2,0,1:T(8,128)(2,1)} %get-tuple-element.162), channel_id=1, source_target_pairs={{0,13},{1,14},{2,15},{3,0},{4,1},{5,2},{6,3},{7,4},{8,5},{9,6},{10... | collective-permute-start | bytes 983048 | tf_op jit(solution)/shard_map/ppermute | solution.py:31
  171.3 22.8 %collective-permute-start.3 = (bf16[1,1,80,2048]{3,2,0,1:T(8,128)(2,1)}, bf16[1,1,80,2048]{3,2,0,1:T(8,128)(2,1)S(1)}, u32[]{:S(2)}, u32[]{:S(2)}) collective-permute-start(bf16[1,1,80,2048]{3,2,0,1:T(8,128)(2,1)} %get-tuple-element.171), channel_id=1, source_target_pairs={{0,4},{1,5},{2,6},{3,7},{4,8},{5,9},{6,10},{7,11},{8,12},{9,13},{1... | collective-permute-start | bytes 983048 | tf_op jit(solution)/shard_map/ppermute | solution.py:31
  178.2 25.9 %collective-permute-start.4 = (bf16[1,1,80,2048]{3,2,0,1:T(8,128)(2,1)}, bf16[1,1,80,2048]{3,2,0,1:T(8,128)(2,1)S(1)}, u32[]{:S(2)}, u32[]{:S(2)}) collective-permute-start(bf16[1,1,80,2048]{3,2,0,1:T(8,128)(2,1)} %get-tuple-element.170), channel_id=1, source_target_pairs={{0,5},{1,6},{2,7},{3,8},{4,9},{5,10},{6,11},{7,12},{8,13},{9,14},{... | collective-permute-start | bytes 983048 | tf_op jit(solution)/shard_map/ppermute | solution.py:31
  194.1 33.2 %collective-permute-start.5 = (bf16[1,1,80,2048]{3,2,0,1:T(8,128)(2,1)}, bf16[1,1,80,2048]{3,2,0,1:T(8,128)(2,1)S(1)}, u32[]{:S(2)}, u32[]{:S(2)}) collective-permute-start(bf16[1,1,80,2048]{3,2,0,1:T(8,128)(2,1)} %get-tuple-element.169), channel_id=1, source_target_pairs={{0,6},{1,7},{2,8},{3,9},{4,10},{5,11},{6,12},{7,13},{8,14},{9,15},... | collective-permute-start | bytes 983048 | tf_op jit(solution)/shard_map/ppermute | solution.py:31
  204.0 30.4 %collective-permute-start.6 = (bf16[1,1,80,2048]{3,2,0,1:T(8,128)(2,1)}, bf16[1,1,80,2048]{3,2,0,1:T(8,128)(2,1)S(1)}, u32[]{:S(2)}, u32[]{:S(2)}) collective-permute-start(bf16[1,1,80,2048]{3,2,0,1:T(8,128)(2,1)} %get-tuple-element.168), channel_id=1, source_target_pairs={{0,7},{1,8},{2,9},{3,10},{4,11},{5,12},{6,13},{7,14},{8,15},{9,0},... | collective-permute-start | bytes 983048 | tf_op jit(solution)/shard_map/ppermute | solution.py:31
  227.3 16.2 %collective-permute-start.7 = (bf16[1,1,80,2048]{3,2,0,1:T(8,128)(2,1)}, bf16[1,1,80,2048]{3,2,0,1:T(8,128)(2,1)S(1)}, u32[]{:S(2)}, u32[]{:S(2)}) collective-permute-start(bf16[1,1,80,2048]{3,2,0,1:T(8,128)(2,1)} %get-tuple-element.167), channel_id=1, source_target_pairs={{0,8},{1,9},{2,10},{3,11},{4,12},{5,13},{6,14},{7,15},{8,0},{9,1},... | collective-permute-start | bytes 983048 | tf_op jit(solution)/shard_map/ppermute | solution.py:31
  234.4 18.3 %collective-permute-start.8 = (bf16[1,1,80,2048]{3,2,0,1:T(8,128)(2,1)}, bf16[1,1,80,2048]{3,2,0,1:T(8,128)(2,1)S(1)}, u32[]{:S(2)}, u32[]{:S(2)}) collective-permute-start(bf16[1,1,80,2048]{3,2,0,1:T(8,128)(2,1)} %get-tuple-element.166), channel_id=1, source_target_pairs={{0,9},{1,10},{2,11},{3,12},{4,13},{5,14},{6,15},{7,0},{8,1},{9,2},... | collective-permute-start | bytes 983048 | tf_op jit(solution)/shard_map/ppermute | solution.py:31
  243.5 23.3 %collective-permute-start.9 = (bf16[1,1,80,2048]{3,2,0,1:T(8,128)(2,1)}, bf16[1,1,80,2048]{3,2,0,1:T(8,128)(2,1)S(1)}, u32[]{:S(2)}, u32[]{:S(2)}) collective-permute-start(bf16[1,1,80,2048]{3,2,0,1:T(8,128)(2,1)} %get-tuple-element.165), channel_id=1, source_target_pairs={{0,10},{1,11},{2,12},{3,13},{4,14},{5,15},{6,0},{7,1},{8,2},{9,3},... | collective-permute-start | bytes 983048 | tf_op jit(solution)/shard_map/ppermute | solution.py:31
  252.8 16.9 %collective-permute-start.10 = (bf16[1,1,80,2048]{3,2,0,1:T(8,128)(2,1)}, bf16[1,1,80,2048]{3,2,0,1:T(8,128)(2,1)S(1)}, u32[]{:S(2)}, u32[]{:S(2)}) collective-permute-start(bf16[1,1,80,2048]{3,2,0,1:T(8,128)(2,1)} %get-tuple-element.164), channel_id=1, source_target_pairs={{0,11},{1,12},{2,13},{3,14},{4,15},{5,0},{6,1},{7,2},{8,3},{9,4},{... | collective-permute-start | bytes 983048 | tf_op jit(solution)/shard_map/ppermute | solution.py:31
  266.8 6.7 %collective-permute-start.11 = (bf16[1,1,80,2048]{3,2,0,1:T(8,128)(2,1)S(1)}, bf16[1,1,80,2048]{3,2,0,1:T(8,128)(2,1)S(1)}, u32[]{:S(2)}, u32[]{:S(2)}) collective-permute-start(bf16[1,1,80,2048]{3,2,0,1:T(8,128)(2,1)S(1)} %copy-done.5), channel_id=1, source_target_pairs={{0,12},{1,13},{2,14},{3,15},{4,0},{5,1},{6,2},{7,3},{8,4},{9,5},{1... | collective-permute-start | bytes 983048 | tf_op jit(solution)/shard_map/ppermute | solution.py:31
  296.2 7.3 %copy-start.4 = (bf16[1280,2048]{1,0:T(8,128)(2,1)S(1)}, bf16[1280,2048]{1,0:T(8,128)(2,1)}, u32[]{:S(2)}) copy-start(bf16[1280,2048]{1,0:T(8,128)(2,1)} %gather_fusion.3) | copy-start | bytes 15728644
  296.2 7.3 %copy-start.12 = (bf16[1,2048,768]{2,1,0:T(8,128)(2,1)S(1)}, bf16[1,2048,768]{2,1,0:T(8,128)(2,1)}, u32[]{:S(2)}) copy-start(bf16[1,2048,768]{2,1,0:T(8,128)(2,1)} %param.22) | copy-start | bytes 9437188
  345.0 127.6 %all-to-all-start.3 = ((bf16[16,80,2048]{2,1,0:T(8,128)(2,1)}), bf16[16,80,2048]{2,1,0:T(8,128)(2,1)}, u32[]{:S(2)}, u32[]{:S(2)}) async-start(bf16[16,80,2048]{2,1,0:T(8,128)(2,1)} %bitcast.125), calls=%async_computation.3 | async-start | bytes 10485760 | tf_op jit(solution)/shard_map/all_to_all | solution.py:191
  472.7 18.3 %copy-start.1 = (bf16[1,768,2048]{2,1,0:T(8,128)(2,1)S(1)}, bf16[1,768,2048]{2,1,0:T(8,128)(2,1)}, u32[]{:S(2)}) copy-start(bf16[1,768,2048]{2,1,0:T(8,128)(2,1)} %param.23) | copy-start | bytes 9437188
  484.9 5.1 %copy-start.3 = (f32[128,2048]{1,0:T(8,128)S(1)}, f32[128,2048]{1,0:T(8,128)}, u32[]{:S(2)}) copy-start(f32[128,2048]{1,0:T(8,128)} %copy-done.2) | copy-start | bytes 3145732
Sparse Core Ops, SparseCore 0:
  8.9 69.4 all-gather.1
